TPU v7x, 32 devices: a whole 2x2x4 slice. The times are simulated.
32 devices in a mesh: pipe: 2 (over core), dp: 4 (over z), tensor: 4 (over y, x).
Axes of the slice: x: 2, y: 2, z: 4, core: 2. Of those that a mesh axis runs over, the one named last changes fastest.
Arguments:
- x_img: bfloat16 [2, 4, 1536, 1024], P(None, 'dp', 'tensor'), may hold values from -6 to 6
- x_txt: bfloat16 [2, 4, 1536, 154], P(None, 'dp', 'tensor'), may hold values from -6 to 6
- cond: bfloat16 [2, 4, 1536], replicated, may hold values from -6 to 6
- cot_img: bfloat16 [2, 4, 1536, 1024], P(None, 'dp', 'tensor'), may hold values from -6 to 6
- cot_txt: bfloat16 [2, 4, 1536, 154], P(None, 'dp', 'tensor'), may hold values from -6 to 6
- ada_img: bfloat16 [2, 1536, 9216], P('pipe', ('dp', 'tensor')), may hold values from -0.15625 to 0.15625
- qkv_img: bfloat16 [2, 3, 4, 384, 1536], P('pipe', None, 'tensor', 'dp'), may hold values from -0.15625 to 0.15625
- proj_img: bfloat16 [2, 4, 384, 1536], P('pipe', 'tensor', 'dp'), may hold values from -0.75 to 0.75
- fc1_img: bfloat16 [2, 1536, 6144], P('pipe', 'dp', 'tensor'), may hold values from -0.15625 to 0.15625
- fc2_img: bfloat16 [2, 1536, 6144], P('pipe', 'dp', 'tensor'), may hold values from -0.078125 to 0.078125
- ada_txt: bfloat16 [2, 1536, 9216], P('pipe', ('dp', 'tensor')), may hold values from -0.15625 to 0.15625
- qkv_txt: bfloat16 [2, 3, 4, 384, 1536], P('pipe', None, 'tensor', 'dp'), may hold values from -0.15625 to 0.15625
- proj_txt: bfloat16 [2, 4, 384, 1536], P('pipe', 'tensor', 'dp'), may hold values from -0.75 to 0.75
- fc1_txt: bfloat16 [2, 1536, 6144], P('pipe', 'dp', 'tensor'), may hold values from -0.15625 to 0.15625
- fc2_txt: bfloat16 [2, 1536, 6144], P('pipe', 'dp', 'tensor'), may hold values from -0.078125 to 0.078125
Outputs:
- section_out_img: bfloat16 [2, 2, 4, 1536, 1024], P('pipe', None, 'dp', 'tensor')
- section_out_txt: bfloat16 [2, 2, 4, 1536, 154], P('pipe', None, 'dp', 'tensor')
- section_grad_img: bfloat16 [2, 2, 4, 1536, 1024], P('pipe', None, 'dp', 'tensor')
- section_grad_txt: bfloat16 [2, 2, 4, 1536, 154], P('pipe', None, 'dp', 'tensor')
- grad_ada_img: float32 [2, 1536, 9216], P('pipe', ('dp', 'tensor'))
- grad_qkv_img: float32 [2, 3, 4, 384, 1536], P('pipe', None, 'tensor', 'dp')
- grad_proj_img: float32 [2, 4, 384, 1536], P('pipe', 'tensor', 'dp')
- grad_fc1_img: float32 [2, 1536, 6144], P('pipe', 'dp', 'tensor')
- grad_fc2_img: float32 [2, 1536, 6144], P('pipe', 'dp', 'tensor')
- grad_ada_txt: float32 [2, 1536, 9216], P('pipe', ('dp', 'tensor'))
- grad_qkv_txt: float32 [2, 3, 4, 384, 1536], P('pipe', None, 'tensor', 'dp')
- grad_proj_txt: float32 [2, 4, 384, 1536], P('pipe', 'tensor', 'dp')
- grad_fc1_txt: float32 [2, 1536, 6144], P('pipe', 'dp', 'tensor')
- grad_fc2_txt: float32 [2, 1536, 6144], P('pipe', 'dp', 'tensor')
All inputs are finite; a program needn't handle non-finite values.
Results may differ from a plain program's by a relative error of at most 0.03.
Values may be sent and summed in bfloat16 or wider, within the bound.
No kernel may reach another device: no remote copies, remote signals or barrier semaphores. Data moves between devices by JAX's collectives and lax.ppermute only.
A program may use at most 640 MiB of HBM per device.

v0:
```python
import jax
import jax.numpy as jnp
from jax import lax
from jax.sharding import PartitionSpec as P

D = 1536
HD = 64
IMG = 1024
MICRO = 2


norm_eps = 1e-06
highest = lax.Precision.HIGHEST


def as_sent(array):
    return jax.tree.map(lambda a: a.astype(jnp.bfloat16) if a.dtype == jnp.float32 else a, array)


def passed_along(array, axis, by):
    peers = lax.axis_size(axis)
    pairs = [(i, i + by) for i in range(peers) if 0 <= i + by < peers]
    return lax.ppermute(array, axis, pairs)


def row_moments(values):
    return lax.psum((values[0], values[1], values[2], values[3]), "tensor")


def widen_rows(shards):
    return jax.tree.map(
        lambda part, own: part.astype(own.dtype),
        lax.all_gather(as_sent(shards), "tensor", axis=1, tiled=True),
        shards,
    )


def narrow(terms):
    return jax.tree.map(
        lambda part: part.astype(jnp.float32),
        lax.psum_scatter(as_sent(terms), "tensor", scatter_dimension=1, tiled=True),
    )


def narrow_grads(terms):
    return jax.tree.map(
        lambda part: part.astype(jnp.float32),
        lax.psum_scatter(as_sent(terms), "tensor", scatter_dimension=1, tiled=True),
    )


def gather_dense(arrays):
    return (
        lax.all_gather(arrays[0], "dp", axis=1, tiled=True),
        lax.all_gather(arrays[1], "dp", axis=0, tiled=True),
        lax.all_gather(arrays[2], "dp", axis=0, tiled=True),
        lax.all_gather(arrays[3], "dp", axis=0, tiled=True),
        lax.all_gather(arrays[4], "dp", axis=1, tiled=True),
        lax.all_gather(arrays[5], "dp", axis=0, tiled=True),
        lax.all_gather(arrays[6], "dp", axis=0, tiled=True),
        lax.all_gather(arrays[7], "dp", axis=0, tiled=True),
    )


def shard_norm(values):
    totals = row_moments(
        (
            jnp.sum(values[0], axis=1, keepdims=True),
            jnp.sum(values[1], axis=1, keepdims=True),
            jnp.sum(values[0] * values[0], axis=1, keepdims=True),
            jnp.sum(values[1] * values[1], axis=1, keepdims=True),
        )
    )
    result = []
    for stream in range(2):
        row_mean = totals[stream] / D
        inverse = lax.rsqrt(totals[stream + 2] / D - row_mean * row_mean + norm_eps)
        result.append((row_mean, inverse))
    return tuple(result)


def apply_norm(values, stats):
    return tuple(((values[stream] - stats[stream][0]) * stats[stream][1] for stream in range(2)))


def modulate(normed, mods, shift_slot, scale_slot):
    return tuple(
        (
            (
                normed[stream] * (1.0 + mods[stream][:, scale_slot]) + mods[stream][:, shift_slot]
            ).astype(jnp.bfloat16)
            for stream in range(2)
        )
    )


def norm_back(grads_in, normed, stats, mods, scale_slot):
    scaled = tuple((grads_in[stream] * (1.0 + mods[stream][:, scale_slot]) for stream in range(2)))
    totals = row_moments(
        (
            jnp.sum(scaled[0], axis=1, keepdims=True),
            jnp.sum(scaled[1], axis=1, keepdims=True),
            jnp.sum(scaled[0] * normed[0], axis=1, keepdims=True),
            jnp.sum(scaled[1] * normed[1], axis=1, keepdims=True),
        )
    )
    return tuple(
        (
            stats[stream][1]
            * (scaled[stream] - totals[stream] / D - normed[stream] * totals[stream + 2] / D)
            for stream in range(2)
        )
    )


def gelu_back(hidden, grad):
    _, pull_back = jax.vjp(lambda value: jax.nn.gelu(value, approximate=True), hidden)
    return pull_back(grad)[0]


def split_heads(joint_qkv):
    return joint_qkv.reshape(joint_qkv.shape[:2] + (-1, HD, joint_qkv.shape[3]))


def attend(joint_qkv):
    shaped = split_heads(joint_qkv)
    inv_root = HD ** (-0.5)
    scores = (
        jnp.einsum("shdq,shdk->shqk", shaped[0], shaped[1], preferred_element_type=jnp.float32)
        * inv_root
    )
    peak_score = jnp.max(scores, axis=-1, keepdims=True)
    log_total = peak_score + jnp.log(jnp.sum(jnp.exp(scores - peak_score), axis=-1, keepdims=True))
    attn_probs = jnp.exp(scores - log_total).astype(jnp.bfloat16)
    mixed_out = jnp.einsum(
        "shqk,shdk->shdq", attn_probs, shaped[2], preferred_element_type=jnp.float32
    )
    return (mixed_out.reshape(joint_qkv.shape[1:]).astype(jnp.bfloat16), log_total)


def attend_back(joint_qkv, log_total, grad_mixed):
    shaped = split_heads(joint_qkv)
    grad_shaped = grad_mixed.reshape(grad_mixed.shape[:1] + (-1, HD, grad_mixed.shape[2]))
    inv_root = HD ** (-0.5)
    scores = (
        jnp.einsum("shdq,shdk->shqk", shaped[0], shaped[1], preferred_element_type=jnp.float32)
        * inv_root
    )
    attn_probs = jnp.exp(scores - log_total)
    grad_probs = jnp.einsum(
        "shdq,shdk->shqk", grad_shaped, shaped[2], preferred_element_type=jnp.float32
    )
    row_dot = jnp.sum(attn_probs * grad_probs, axis=-1, keepdims=True)
    grad_scores = (attn_probs * (grad_probs - row_dot)).astype(jnp.bfloat16)
    grad_query = (
        jnp.einsum("shqk,shdk->shdq", grad_scores, shaped[1], preferred_element_type=jnp.float32)
        * inv_root
    )
    grad_key = (
        jnp.einsum("shqk,shdq->shdk", grad_scores, shaped[0], preferred_element_type=jnp.float32)
        * inv_root
    )
    grad_value = jnp.einsum(
        "shqk,shdq->shdk",
        attn_probs.astype(jnp.bfloat16),
        grad_shaped,
        preferred_element_type=jnp.float32,
    )
    return (
        jnp.stack([grad_query, grad_key, grad_value]).reshape(joint_qkv.shape).astype(jnp.bfloat16)
    )


def fold_back(shards, weights, lefts, totals, row_major):
    empty = []
    for stream in range(2):
        inner_width = weights[stream].shape[1] if row_major else weights[stream].shape[0]
        empty.append(
            jnp.zeros((shards[stream].shape[0], inner_width, shards[stream].shape[2]), jnp.float32)
        )
    pieces = jax.tree.map(
        lambda part: lax.all_gather(part, "tensor", axis=1, tiled=True), as_sent(shards)
    )
    new_sums = []
    new_grads = []
    for stream in range(2):
        if row_major:
            rows = weights[stream]
            new_sums.append(
                jnp.einsum("srl,rf->sfl", pieces[stream], rows, preferred_element_type=jnp.float32)
            )
            grad_block = totals[stream]
            grad_block = grad_block + jnp.einsum(
                "sfl,srl->rf", lefts[stream], pieces[stream], preferred_element_type=jnp.float32
            )
            new_grads.append(grad_block)
        else:
            columns = weights[stream]
            new_sums.append(
                jnp.einsum(
                    "srl,er->sel", pieces[stream], columns, preferred_element_type=jnp.float32
                )
            )
            grad_block = totals[stream]
            grad_block = grad_block + jnp.einsum(
                "sel,srl->er", lefts[stream], pieces[stream], preferred_element_type=jnp.float32
            )
            new_grads.append(grad_block)
    return (tuple(new_sums), tuple(new_grads))


def local_mods(modulation, micro_index, column, local_width):
    current = lax.dynamic_index_in_dim(modulation, micro_index, 0, keepdims=False)
    result = []
    for stream in range(2):
        whole_mod = current[:, stream].reshape(current.shape[0], 6, D)
        result.append(
            lax.dynamic_slice_in_dim(whole_mod, column * local_width, local_width, 2)[..., None]
        )
    return tuple(result)


def forward_section(inputs, mods, dense_w):
    residual = tuple((value.astype(jnp.float32) for value in inputs))
    stats_in = shard_norm(residual)
    norm_in = widen_rows(modulate(apply_norm(residual, stats_in), mods, 0, 1))
    triples = tuple(
        (
            jnp.einsum(
                "sdl,ced->csel",
                norm_in[stream],
                dense_w[stream][0],
                preferred_element_type=jnp.float32,
            ).astype(jnp.bfloat16)
            for stream in range(2)
        )
    )
    joint_qkv = jnp.concatenate(triples, axis=3)
    mixed_out, log_total = attend(joint_qkv)
    split_mixed = (mixed_out[:, :, :IMG], mixed_out[:, :, IMG:])
    attn_out = narrow(
        tuple(
            (
                jnp.einsum(
                    "sel,ed->sdl",
                    split_mixed[stream],
                    dense_w[stream][1],
                    preferred_element_type=jnp.float32,
                )
                for stream in range(2)
            )
        )
    )
    middle = tuple(
        (residual[stream] + mods[stream][:, 2] * attn_out[stream] for stream in range(2))
    )
    stats_mid = shard_norm(middle)
    norm_mid = widen_rows(modulate(apply_norm(middle, stats_mid), mods, 3, 4))
    hidden = tuple(
        (
            jnp.einsum(
                "sdl,df->sfl",
                norm_mid[stream],
                dense_w[stream][2],
                preferred_element_type=jnp.float32,
            )
            for stream in range(2)
        )
    )
    active = tuple(
        (jax.nn.gelu(hidden[stream], approximate=True).astype(jnp.bfloat16) for stream in range(2))
    )
    branch = narrow(
        tuple(
            (
                jnp.einsum(
                    "sfl,df->sdl",
                    active[stream],
                    dense_w[stream][3],
                    preferred_element_type=jnp.float32,
                )
                for stream in range(2)
            )
        )
    )
    result = tuple(
        (
            (middle[stream] + mods[stream][:, 5] * branch[stream]).astype(jnp.bfloat16)
            for stream in range(2)
        )
    )
    stash_now = (
        inputs,
        attn_out,
        branch,
        stats_in,
        stats_mid,
        norm_in,
        norm_mid,
        joint_qkv,
        mixed_out,
        log_total,
        hidden,
        active,
    )
    return (result, stash_now)


def backward_section(stash_now, mods, dense_w, grad_out, grad_acc):
    (
        inputs,
        attn_out,
        branch,
        stats_in,
        stats_mid,
        norm_in,
        norm_mid,
        joint_qkv,
        mixed_out,
        log_total,
        hidden,
        active,
    ) = stash_now
    residual = tuple((value.astype(jnp.float32) for value in inputs))
    normed_in = apply_norm(residual, stats_in)
    middle = tuple(
        (residual[stream] + mods[stream][:, 2] * attn_out[stream] for stream in range(2))
    )
    normed_mid = apply_norm(middle, stats_mid)
    grad_branch = tuple(
        ((mods[stream][:, 5] * grad_out[stream]).astype(jnp.bfloat16) for stream in range(2))
    )
    gate_two = tuple((jnp.sum(grad_out[stream] * branch[stream], axis=2) for stream in range(2)))
    grad_active, fc2_grads = fold_back(
        grad_branch, (dense_w[0][3], dense_w[1][3]), active, (grad_acc[0][3], grad_acc[1][3]), True
    )
    grad_hidden = tuple(
        (gelu_back(hidden[stream], grad_active[stream]).astype(jnp.bfloat16) for stream in range(2))
    )
    fc1_grads = tuple(
        (
            grad_acc[stream][2]
            + jnp.einsum(
                "sdl,sfl->df",
                norm_mid[stream],
                grad_hidden[stream],
                preferred_element_type=jnp.float32,
            )
            for stream in range(2)
        )
    )
    grad_mid_in = narrow_grads(
        tuple(
            (
                jnp.einsum(
                    "sfl,df->sdl",
                    grad_hidden[stream],
                    dense_w[stream][2],
                    preferred_element_type=jnp.float32,
                )
                for stream in range(2)
            )
        )
    )
    shift_two = tuple((jnp.sum(grad_mid_in[stream], axis=2) for stream in range(2)))
    scale_two = tuple(
        (jnp.sum(grad_mid_in[stream] * normed_mid[stream], axis=2) for stream in range(2))
    )
    back_mid = norm_back(grad_mid_in, normed_mid, stats_mid, mods, 4)
    grad_middle = tuple((grad_out[stream] + back_mid[stream] for stream in range(2)))
    grad_attn = tuple(
        ((mods[stream][:, 2] * grad_middle[stream]).astype(jnp.bfloat16) for stream in range(2))
    )
    gate_one = tuple(
        (jnp.sum(grad_middle[stream] * attn_out[stream], axis=2) for stream in range(2))
    )
    split_mixed = (mixed_out[:, :, :IMG], mixed_out[:, :, IMG:])
    grad_split, proj_grads = fold_back(
        grad_attn,
        (dense_w[0][1], dense_w[1][1]),
        split_mixed,
        (grad_acc[0][1], grad_acc[1][1]),
        False,
    )
    grad_mixed = jnp.concatenate(grad_split, axis=2).astype(jnp.bfloat16)
    grad_joint = attend_back(joint_qkv, log_total, grad_mixed)
    grad_triples = (grad_joint[..., :IMG], grad_joint[..., IMG:])
    qkv_grads = tuple(
        (
            grad_acc[stream][0]
            + jnp.einsum(
                "sdl,csel->ced",
                norm_in[stream],
                grad_triples[stream],
                preferred_element_type=jnp.float32,
            )
            for stream in range(2)
        )
    )
    grad_in_norm = narrow_grads(
        tuple(
            (
                jnp.einsum(
                    "csel,ced->sdl",
                    grad_triples[stream],
                    dense_w[stream][0],
                    preferred_element_type=jnp.float32,
                )
                for stream in range(2)
            )
        )
    )
    shift_one = tuple((jnp.sum(grad_in_norm[stream], axis=2) for stream in range(2)))
    scale_one = tuple(
        (jnp.sum(grad_in_norm[stream] * normed_in[stream], axis=2) for stream in range(2))
    )
    back_in = norm_back(grad_in_norm, normed_in, stats_in, mods, 1)
    grad_input = tuple((grad_middle[stream] + back_in[stream] for stream in range(2)))
    mod_grads = tuple(
        (
            jnp.stack(
                [
                    shift_one[stream],
                    scale_one[stream],
                    gate_one[stream],
                    shift_two[stream],
                    scale_two[stream],
                    gate_two[stream],
                ],
                axis=1,
            )
            for stream in range(2)
        )
    )
    new_acc = tuple(
        (
            (qkv_grads[stream], proj_grads[stream], fc1_grads[stream], fc2_grads[stream])
            for stream in range(2)
        )
    )
    return (grad_input, mod_grads, new_acc)


def local(
    x_img,
    x_txt,
    cond,
    cot_img,
    cot_txt,
    ada_img,
    qkv_img,
    proj_img,
    fc1_img,
    fc2_img,
    ada_txt,
    qkv_txt,
    proj_txt,
    fc1_txt,
    fc2_txt,
):
    section_index = lax.axis_index("pipe")
    head_section = section_index == 0
    tail_section = section_index == lax.axis_size("pipe") - 1
    tick_count = MICRO + lax.axis_size("pipe") - 1
    column = lax.axis_index("tensor")
    dp_index = lax.axis_index("dp")
    seq_count = x_img.shape[1]
    local_width = x_img.shape[2]
    row_count = ada_img.shape[1]
    silu_all = jax.nn.silu(cond.astype(jnp.float32)).astype(jnp.bfloat16)
    silu_own = lax.dynamic_slice_in_dim(silu_all, dp_index * seq_count, seq_count, 1).reshape(
        MICRO * seq_count, D
    )
    cond_cols = silu_own
    modulation = jnp.stack(
        [
            jnp.dot(
                cond_cols,
                lax.all_gather(ada_img[0], ("dp", "tensor"), axis=0, tiled=True),
                preferred_element_type=jnp.float32,
            ),
            jnp.dot(
                cond_cols,
                lax.all_gather(ada_txt[0], ("dp", "tensor"), axis=0, tiled=True),
                preferred_element_type=jnp.float32,
            ),
        ],
        axis=1,
    )
    modulation = modulation.reshape(MICRO, seq_count, 2, 6 * D)
    local_w = (
        qkv_img[0, :, 0],
        proj_img[0, 0],
        fc1_img[0],
        fc2_img[0],
        qkv_txt[0, :, 0],
        proj_txt[0, 0],
        fc1_txt[0],
        fc2_txt[0],
    )
    gathered = gather_dense(local_w)
    dense_w = (gathered[:4], gathered[4:])
    received = (jnp.zeros(x_img.shape[1:], jnp.bfloat16), jnp.zeros(x_txt.shape[1:], jnp.bfloat16))
    stash_list = []
    out_list = []
    for fwd_tick in range(tick_count):
        micro_index = jnp.clip(fwd_tick - section_index, 0, MICRO - 1)
        own_slot = min(fwd_tick, MICRO - 1)
        entry = (
            jnp.where(head_section, x_img[own_slot], received[0]),
            jnp.where(head_section, x_txt[own_slot], received[1]),
        )
        mods = local_mods(modulation, micro_index, column, local_width)
        result, stash_now = forward_section(entry, mods, dense_w)
        stash_list.append((stash_now, mods, micro_index))
        out_list.append(result)
        if fwd_tick + 1 < tick_count:
            received = jax.tree.map(
                lambda part, own: part.astype(own.dtype),
                passed_along(as_sent(result), "pipe", 1),
                result,
            )
    gathered = gather_dense(local_w)
    dense_w = (gathered[:4], gathered[4:])
    grad_acc = tuple(
        (
            tuple((jnp.zeros(matrix.shape, jnp.float32) for matrix in dense_w[stream]))
            for stream in range(2)
        )
    )
    mod_grad_acc = jnp.zeros((MICRO, seq_count, 2, 6, local_width), jnp.float32)
    received = (jnp.zeros(x_img.shape[1:], jnp.bfloat16), jnp.zeros(x_txt.shape[1:], jnp.bfloat16))
    grad_list = []
    for back_turn in range(tick_count):
        fwd_tick = tick_count - 1 - back_turn
        stash_now, mods, micro_index = stash_list[fwd_tick]
        micro_raw = fwd_tick - section_index
        live_flag = ((micro_raw >= 0) & (micro_raw < MICRO)).astype(jnp.float32)
        cot_slot = min(max(MICRO - 1 - back_turn, 0), MICRO - 1)
        grad_out = (
            jnp.where(tail_section, cot_img[cot_slot], received[0]).astype(jnp.float32) * live_flag,
            jnp.where(tail_section, cot_txt[cot_slot], received[1]).astype(jnp.float32) * live_flag,
        )
        grad_input, mod_grads, grad_acc = backward_section(
            stash_now, mods, dense_w, grad_out, grad_acc
        )
        picker = (jnp.arange(MICRO) == micro_index).astype(jnp.float32)
        mod_grad_acc = (
            mod_grad_acc + picker[:, None, None, None, None] * jnp.stack(mod_grads, axis=1)[None]
        )
        grad_half = tuple((value.astype(jnp.bfloat16) for value in grad_input))
        grad_list.append(grad_half)
        if back_turn + 1 < tick_count:
            received = jax.tree.map(
                lambda part, own: part.astype(own.dtype),
                passed_along(as_sent(grad_half), "pipe", -1),
                grad_half,
            )
    flat_grads = grad_acc[0] + grad_acc[1]
    summed = (
        lax.psum_scatter(
            flat_grads[0].astype(jnp.bfloat16), "dp", scatter_dimension=1, tiled=True
        ).astype(jnp.float32),
        lax.psum_scatter(
            flat_grads[1].astype(jnp.bfloat16), "dp", scatter_dimension=0, tiled=True
        ).astype(jnp.float32),
        lax.psum_scatter(
            flat_grads[2].astype(jnp.bfloat16), "dp", scatter_dimension=0, tiled=True
        ).astype(jnp.float32),
        lax.psum_scatter(
            flat_grads[3].astype(jnp.bfloat16), "dp", scatter_dimension=0, tiled=True
        ).astype(jnp.float32),
        lax.psum_scatter(
            flat_grads[4].astype(jnp.bfloat16), "dp", scatter_dimension=1, tiled=True
        ).astype(jnp.float32),
        lax.psum_scatter(
            flat_grads[5].astype(jnp.bfloat16), "dp", scatter_dimension=0, tiled=True
        ).astype(jnp.float32),
        lax.psum_scatter(
            flat_grads[6].astype(jnp.bfloat16), "dp", scatter_dimension=0, tiled=True
        ).astype(jnp.float32),
        lax.psum_scatter(
            flat_grads[7].astype(jnp.bfloat16), "dp", scatter_dimension=0, tiled=True
        ).astype(jnp.float32),
    )
    flat_mod = mod_grad_acc.reshape(MICRO * seq_count, 2, 6, local_width)
    cond_cols = silu_own.astype(jnp.float32)
    local_term = jnp.einsum("br,bkcf->rkcf", cond_cols, flat_mod, precision=highest)
    whole_term = jnp.zeros((row_count * lax.axis_size(("dp", "tensor")), 2, 6, D), jnp.float32)
    whole_term = lax.dynamic_update_slice_in_dim(whole_term, local_term, column * local_width, 3)
    ada_grad = lax.psum_scatter(
        whole_term.reshape(row_count * lax.axis_size(("dp", "tensor")), 12 * D),
        ("dp", "tensor"),
        scatter_dimension=0,
        tiled=True,
    )
    section_out_img = jnp.stack(
        [
            jnp.where(head_section, out_list[micro][0], out_list[micro + 1][0])
            for micro in range(MICRO)
        ]
    )[None]
    section_out_txt = jnp.stack(
        [
            jnp.where(head_section, out_list[micro][1], out_list[micro + 1][1])
            for micro in range(MICRO)
        ]
    )[None]
    section_grad_img = jnp.stack(
        [
            jnp.where(head_section, grad_list[MICRO - micro][0], grad_list[MICRO - 1 - micro][0])
            for micro in range(MICRO)
        ]
    )[None]
    section_grad_txt = jnp.stack(
        [
            jnp.where(head_section, grad_list[MICRO - micro][1], grad_list[MICRO - 1 - micro][1])
            for micro in range(MICRO)
        ]
    )[None]
    return (
        section_out_img,
        section_out_txt,
        section_grad_img,
        section_grad_txt,
        ada_grad[:, : 6 * D][None],
        summed[0][None, :, None],
        summed[1][None, None],
        summed[2][None],
        summed[3][None],
        ada_grad[:, 6 * D :][None],
        summed[4][None, :, None],
        summed[5][None, None],
        summed[6][None],
        summed[7][None],
    )


def solution(mesh):
    return jax.shard_map(
        local,
        mesh=mesh,
        in_specs=(
            P(None, "dp", "tensor", None),
            P(None, "dp", "tensor", None),
            P(),
            P(None, "dp", "tensor", None),
            P(None, "dp", "tensor", None),
            P("pipe", ("dp", "tensor"), None),
            P("pipe", None, "tensor", "dp", None),
            P("pipe", "tensor", "dp", None),
            P("pipe", "dp", "tensor"),
            P("pipe", "dp", "tensor"),
            P("pipe", ("dp", "tensor"), None),
            P("pipe", None, "tensor", "dp", None),
            P("pipe", "tensor", "dp", None),
            P("pipe", "dp", "tensor"),
            P("pipe", "dp", "tensor"),
        ),
        out_specs=(
            P("pipe", None, "dp", "tensor", None),
            P("pipe", None, "dp", "tensor", None),
            P("pipe", None, "dp", "tensor", None),
            P("pipe", None, "dp", "tensor", None),
            P("pipe", ("dp", "tensor"), None),
            P("pipe", None, "tensor", "dp", None),
            P("pipe", "tensor", "dp", None),
            P("pipe", "dp", "tensor"),
            P("pipe", "dp", "tensor"),
            P("pipe", ("dp", "tensor"), None),
            P("pipe", None, "tensor", "dp", None),
            P("pipe", "tensor", "dp", None),
            P("pipe", "dp", "tensor"),
            P("pipe", "dp", "tensor"),
        ),
        check_vma=False,
    )
```

profile of v0, /device:TPU:0, one launch (start us, length us, event | category | flops | bytes accessed | tf_op | source)
XLA Modules:
  0.0 5541.5 jit_solution(6224098616269169446)
XLA Ops:
  31.4 282.4 %all-gather.59.cloned.1.call-done = bf16[1,1536,9216]{2,1,0:T(8,128)(2,1)} async-done(((bf16[1,96,9216]{2,1,0:T(8,128)(2,1)}), bf16[1,1536,9216]{2,1,0:T(8,128)(2,1)}) %all-gather.59.cloned.1.call-update) | async-done | bytes 28311568 | tf_op jit(solution)/shard_map/all_gather | solution.py:484
  325.0 290.0 %all-gather.57.cloned.1.call-done = bf16[1,1536,9216]{2,1,0:T(8,128)(2,1)} async-done(((bf16[1,96,9216]{2,1,0:T(8,128)(2,1)}), bf16[1,1536,9216]{2,1,0:T(8,128)(2,1)}) %all-gather.57.cloned.1.call-update) | async-done | bytes 28311568 | tf_op jit(solution)/shard_map/all_gather | solution.py:479
  643.5 41.3 all-gather.63.cloned.1.call-done
  688.0 66.7 %all-gather.61.cloned.1.call-done = bf16[1,3,1,384,1536]{4,3,1,2,0:T(8,128)(2,1)} async-done(((bf16[1,3,1,96,1536]{4,3,1,2,0:T(8,128)(2,1)}), bf16[1,3,1,384,1536]{4,3,1,2,0:T(8,128)(2,1)}) %all-gather.61.cloned.1.call-update) | async-done | bytes 3538960 | tf_op jit(solution)/shard_map/all_gather | solution.py:54
  754.7 44.6 all-gather.33.cloned.1.call-done
  892.9 45.5 reduce-scatter.100.cloned.1.call-done
  960.8 68.5 %all-gather.67.cloned.1.call-done = bf16[1,1536,1536]{2,1,0:T(8,128)(2,1)} async-done(((bf16[1,384,1536]{2,1,0:T(8,128)(2,1)}), bf16[1,1536,1536]{2,1,0:T(8,128)(2,1)}) %all-gather.67.cloned.1.call-update) | async-done | bytes 4718608 | tf_op jit(solution)/shard_map/all_gather | solution.py:56
  1029.3 44.6 all-gather.35.cloned.1.call-done
  1083.6 81.2 %all-gather.69.cloned.1.call-done = bf16[1,1536,1536]{2,1,0:T(8,128)(2,1)} async-done(((bf16[1,384,1536]{2,1,0:T(8,128)(2,1)}), bf16[1,1536,1536]{2,1,0:T(8,128)(2,1)}) %all-gather.69.cloned.1.call-update) | async-done | bytes 4718608 | tf_op jit(solution)/shard_map/all_gather | solution.py:57
  1208.1 46.1 all-gather.73.cloned.1.call-done
  1257.4 86.0 %all-gather.75.cloned.1.call-done = bf16[1,1536,1536]{2,1,0:T(8,128)(2,1)} async-done(((bf16[1,384,1536]{2,1,0:T(8,128)(2,1)}), bf16[1,1536,1536]{2,1,0:T(8,128)(2,1)}) %all-gather.75.cloned.1.call-update) | async-done | bytes 4718608 | tf_op jit(solution)/shard_map/all_gather | solution.py:61
  1597.7 41.4 reduce-scatter.108.cloned.1.call-done
  1669.7 43.8 all-gather.39.cloned.1.call-done
  2001.0 44.9 reduce-scatter.116.cloned.1.call-done
  2526.7 38.4 reduce-scatter.128.cloned.1.call-done
  2703.0 38.4 reduce-scatter.130.cloned.1.call-done
  2975.2 38.4 reduce-scatter.136.cloned.1.call-done
  3150.7 38.4 reduce-scatter.138.cloned.1.call-done
  3590.4 109.7 %copy.278 = f32[1536,18432]{1,0:T(8,128)} copy(f32[1536,18432]{0,1:T(8,128)} %bitcast.275) | data formatting | bytes 226492416
  3715.2 38.9 reduce-scatter.90.cloned.1.call-done
  3757.1 85.0 %reduce-scatter.88.cloned.1.call-done = bf16[384,1536]{1,0:T(8,128)(2,1)} async-done(((bf16[1536,1536]{1,0:T(8,128)(2,1)}), bf16[384,1536]{1,0:T(8,128)(2,1)}) %reduce-scatter.88.cloned.1.call-update) | async-done | bytes 1179664 | tf_op jit(solution)/shard_map/reduce_scatter | solution.py:567
  3900.9 41.8 reduce-scatter.92.cloned.1.call-done
  3945.4 67.0 %reduce-scatter.84.cloned.1.call-done = bf16[3,96,1536]{2,1,0:T(8,128)(2,1)} async-done(((bf16[3,384,1536]{2,1,0:T(8,128)(2,1)}), bf16[3,96,1536]{2,1,0:T(8,128)(2,1)}) %reduce-scatter.84.cloned.1.call-update) | async-done | bytes 884752 | tf_op jit(solution)/shard_map/reduce_scatter | solution.py:561
  4015.0 1493.8 %reduce-scatter.148.cloned.1.call-done = f32[96,18432]{1,0:T(8,128)} async-done(((f32[1536,18432]{1,0:T(8,128)}), f32[96,18432]{1,0:T(8,128)}) %reduce-scatter.148.cloned.1.call-update) | async-done | bytes 7077904
  (1134 shorter events, 2305.8 us)
Async XLA Ops:
  7.2 306.6 %all-gather.59.cloned.1.call-start = ((), (), s32[]{:S(2)}) async-start(), calls=%async_computation.54 | async-start | bytes 30081024 | tf_op jit(solution)/shard_map/all_gather | solution.py:484
  7.9 607.1 %all-gather.57.cloned.1.call-start = ((), (), s32[]{:S(2)}) async-start(), calls=%async_computation.53 | async-start | bytes 30081024 | tf_op jit(solution)/shard_map/all_gather | solution.py:479
  8.7 676.1 %all-gather.63.cloned.1.call-start = ((), (), s32[]{:S(2)}) async-start(), calls=%async_computation.56 | async-start | bytes 4423680 | tf_op jit(solution)/shard_map/all_gather | solution.py:58
  9.4 745.3 %all-gather.61.cloned.1.call-start = ((), (), s32[]{:S(2)}) async-start(), calls=%async_computation.55 | async-start | bytes 4423680 | tf_op jit(solution)/shard_map/all_gather | solution.py:54
  10.0 789.3 %all-gather.33.cloned.1.call-start = ((), (), s32[]{:S(2)}) async-start(), calls=%async_computation.33 | async-start | bytes 3932160 | tf_op jit(solution)/shard_map/all_gather | solution.py:33
  629.8 225.3 %all-gather.71.cloned.1.call-start = ((), (), s32[]{:S(2)}) async-start(), calls=%async_computation.60 | async-start | bytes 1474560 | tf_op jit(solution)/shard_map/all_gather | solution.py:59
  630.4 233.0 %all-gather.65.cloned.1.call-start = ((), (), s32[]{:S(2)}) async-start(), calls=%async_computation.57 | async-start | bytes 1474560 | tf_op jit(solution)/shard_map/all_gather | solution.py:55
  631.2 259.8 %reduce-scatter.104.cloned.1.call-start = ((), (), s32[]{:S(2)}) async-start(), calls=%async_computation.65 | async-start | bytes 983040
  958.8 205.9 %all-gather.69.cloned.1.call-start = ((), (), s32[]{:S(2)}) async-start(), calls=%async_computation.59 | async-start | bytes 5898240 | tf_op jit(solution)/shard_map/all_gather | solution.py:57
  959.4 294.7 %all-gather.73.cloned.1.call-start = ((), (), s32[]{:S(2)}) async-start(), calls=%async_computation.61 | async-start | bytes 5898240 | tf_op jit(solution)/shard_map/all_gather | solution.py:60
  960.2 383.2 %all-gather.75.cloned.1.call-start = ((), (), s32[]{:S(2)}) async-start(), calls=%async_computation.62 | async-start | bytes 5898240 | tf_op jit(solution)/shard_map/all_gather | solution.py:61
  960.8 428.4 %reduce-scatter.102.cloned.1.call-start = ((), (), s32[]{:S(2)}) async-start(), calls=%async_computation.64 | async-start | bytes 3932160
  1196.2 222.4 %reduce-scatter.106.cloned.1.call-start = ((), (), s32[]{:S(2)}) async-start(), calls=%async_computation.66 | async-start | bytes 983040
  2774.7 195.0 %reduce-scatter.140.cloned.1.call-start = ((), (), s32[]{:S(2)}) async-start(), calls=%async_computation.83 | async-start | bytes 983040
  3222.4 305.8 %reduce-scatter.146.cloned.1.call-start = ((), (), s32[]{:S(2)}) async-start(), calls=%async_computation.86 | async-start | bytes 983040
  3411.4 296.0 %reduce-scatter.98.cloned.1.call-start = ((), (), s32[]{:S(2)}) async-start(), calls=%async_computation.52 | async-start | bytes 5898240 | tf_op jit(solution)/shard_map/reduce_scatter | solution.py:582
  3419.5 290.9 %reduce-scatter.96.cloned.1.call-start = ((), (), s32[]{:S(2)}) async-start(), calls=%async_computation.51 | async-start | bytes 5898240 | tf_op jit(solution)/shard_map/reduce_scatter | solution.py:579
  3427.2 286.2 %reduce-scatter.94.cloned.1.call-start = ((), (), s32[]{:S(2)}) async-start(), calls=%async_computation.50 | async-start | bytes 1474560 | tf_op jit(solution)/shard_map/reduce_scatter | solution.py:576
  3442.6 311.5 %reduce-scatter.90.cloned.1.call-start = ((), (), s32[]{:S(2)}) async-start(), calls=%async_computation.48 | async-start | bytes 5898240 | tf_op jit(solution)/shard_map/reduce_scatter | solution.py:570
  3464.3 377.8 %reduce-scatter.88.cloned.1.call-start = ((), (), s32[]{:S(2)}) async-start(), calls=%async_computation.47 | async-start | bytes 5898240 | tf_op jit(solution)/shard_map/reduce_scatter | solution.py:567
  3491.5 383.4 %reduce-scatter.86.cloned.1.call-start = ((), (), s32[]{:S(2)}) async-start(), calls=%async_computation.46 | async-start | bytes 1474560 | tf_op jit(solution)/shard_map/reduce_scatter | solution.py:564
  3499.5 443.3 %reduce-scatter.92.cloned.1.call-start = ((), (), s32[]{:S(2)}) async-start(), calls=%async_computation.49 | async-start | bytes 4423680 | tf_op jit(solution)/shard_map/reduce_scatter | solution.py:573
  3504.9 507.5 %reduce-scatter.84.cloned.1.call-start = ((), (), s32[]{:S(2)}) async-start(), calls=%async_computation.45 | async-start | bytes 4423680 | tf_op jit(solution)/shard_map/reduce_scatter | solution.py:561
  3527.0 1981.8 %reduce-scatter.148.cloned.1.call-start = ((), (), s32[]{:S(2)}) async-start(), calls=%async_computation.87 | async-start | bytes 120324096
  (303 other events, 17929.4 us)
Sparse Core Ops, SparseCore 0:
  10.8 302.9 all-gather.58
  316.6 298.3 all-gather.56
  616.6 68.1 all-gather.62
  686.2 68.4 all-gather.60
  939.9 89.3 all-gather.66
  1075.3 89.3 all-gather.68
  1166.3 87.7 all-gather.72
  1255.6 87.7 all-gather.74
  1447.9 44.5 all-gather.36
  1754.8 47.3 reduce-scatter.109
  1866.1 45.0 all-gather.40
  2069.6 48.4 all-gather.42
  2330.8 44.5 all-gather.46
  2605.4 48.1 all-gather.48
  2774.8 45.0 all-gather.50
  3054.0 47.2 all-gather.52
  3222.5 45.1 all-gather.54
  3462.0 85.2 reduce-scatter.97
  3549.4 85.7 reduce-scatter.95
  3670.2 83.8 reduce-scatter.89
  3756.3 85.7 reduce-scatter.87
  3877.6 65.0 reduce-scatter.91
  3945.7 66.6 reduce-scatter.83
  4018.4 1490.3 reduce-scatter.147
  (31 shorter events, 1084.0 us)
where the time goes:
time: 5560 us; the launch traced here: 5540 us
  waiting for transfers between devices  3430 us (62%)
  local copies, waits for them, and re-layouts  734 us (13%)
  matrix products  687 us (12%)
  blocking collectives  361 us (6%)
  other arithmetic  292 us (5%)
    unnamed x80, waiting for transfers between devices  1900 us
    unnamed x637, local copies, waits for them, and re-layouts  642 us
    all_gather x1, waiting for transfers between devices, local(): lax.all_gather(ada_img[0], ('dp', 'tensor'), axis=0, tiled=True)  290 us
    all_gather x1, waiting for transfers between devices, local(): lax.all_gather(ada_txt[0], ('dp', 'tensor'), axis=0, tiled=True)  282 us
    psum x12, blocking collectives, row_moments(): return lax.psum((values[0], values[1], values[2], values[3]), 'tensor')  194 us
    all_gather x6, waiting for transfers between devices, widen_rows(): lax.all_gather(as_sent(shards), 'tensor', axis=1, tiled=True)  179 us
    all_gather x6, waiting for transfers between devices, fold_back(): lax.all_gather(part, 'tensor', axis=1, tiled=True)  117 us
  transfers between devices with their start and end apart: 63, of which 44 were waited for; matrix products, arithmetic and copies ran while one was open for 18% of the time, Pallas kernels for 0%

commit v1 on v0

--- a/solution.py
+++ b/solution.py
@@ -468,24 +468,20 @@
     local_width = x_img.shape[2]
     row_count = ada_img.shape[1]
     silu_all = jax.nn.silu(cond.astype(jnp.float32)).astype(jnp.bfloat16)
-    silu_own = lax.dynamic_slice_in_dim(silu_all, dp_index * seq_count, seq_count, 1).reshape(
-        MICRO * seq_count, D
-    )
-    cond_cols = silu_own
-    modulation = jnp.stack(
+    dp_size = lax.axis_size("dp")
+    row_start = (dp_index * lax.axis_size("tensor") + column) * row_count
+    silu_rows = lax.dynamic_slice_in_dim(
+        silu_all.reshape(-1, D), row_start, row_count, 1
+    )
+    partial_mods = jnp.concatenate(
         [
-            jnp.dot(
-                cond_cols,
-                lax.all_gather(ada_img[0], ("dp", "tensor"), axis=0, tiled=True),
-                preferred_element_type=jnp.float32,
-            ),
-            jnp.dot(
-                cond_cols,
-                lax.all_gather(ada_txt[0], ("dp", "tensor"), axis=0, tiled=True),
-                preferred_element_type=jnp.float32,
-            ),
+            jnp.dot(silu_rows, ada_img[0], preferred_element_type=jnp.float32),
+            jnp.dot(silu_rows, ada_txt[0], preferred_element_type=jnp.float32),
         ],
         axis=1,
+    ).reshape(MICRO, dp_size * seq_count, 12 * D)
+    modulation = lax.psum(
+        lax.psum_scatter(partial_mods, "dp", scatter_dimension=1, tiled=True), "tensor"
     )
     modulation = modulation.reshape(MICRO, seq_count, 2, 6 * D)
     local_w = (
@@ -583,16 +579,13 @@
             flat_grads[7].astype(jnp.bfloat16), "dp", scatter_dimension=0, tiled=True
         ).astype(jnp.float32),
     )
-    flat_mod = mod_grad_acc.reshape(MICRO * seq_count, 2, 6, local_width)
-    cond_cols = silu_own.astype(jnp.float32)
-    local_term = jnp.einsum("br,bkcf->rkcf", cond_cols, flat_mod, precision=highest)
-    whole_term = jnp.zeros((row_count * lax.axis_size(("dp", "tensor")), 2, 6, D), jnp.float32)
-    whole_term = lax.dynamic_update_slice_in_dim(whole_term, local_term, column * local_width, 3)
-    ada_grad = lax.psum_scatter(
-        whole_term.reshape(row_count * lax.axis_size(("dp", "tensor")), 12 * D),
-        ("dp", "tensor"),
-        scatter_dimension=0,
-        tiled=True,
+    every_mod = lax.all_gather(mod_grad_acc, ("dp", "tensor"), axis=0, tiled=False)
+    every_mod = every_mod.reshape(
+        (dp_size, lax.axis_size("tensor"), MICRO, seq_count, 12, local_width)
+    )
+    flat_mod = every_mod.transpose(2, 0, 3, 4, 1, 5).reshape(-1, 12 * D)
+    ada_grad = jnp.einsum(
+        "br,bf->rf", silu_rows.astype(jnp.float32), flat_mod, precision=highest
     )
     section_out_img = jnp.stack(
         [

time: 5560 us -> 3370 us (0.61)
  waiting for transfers between devices: 3430 us -> 1480 us
  local copies, waits for them, and re-layouts: 734 us -> 535 us
    unnamed x80 -> x79, waiting for transfers between devices: 1900 us -> 527 us
    all_gather x2 -> x0, waiting for transfers between devices: 572 us -> none  [the longest x1 290 us: local(): lax.all_gather(ada_img[0], ('dp', 'tensor'), axis=0, tiled=True)]
    unnamed x637 -> x722, local copies, waits for them, and re-layouts: 642 us -> 483 us
    reduce_scatter x1, waiting for transfers between devices: 67 us -> 0.01 us  [local(): lax.psum_scatter(flat_grads[0].astype(jnp.bfloat16), 'dp', scatter_dimens...]
  transfers between devices with their start and end apart: 63 -> 62, of which waited for: 44 -> 43; matrix products, arithmetic and copies ran while one was open for 18% -> 28% of each run, Pallas kernels for 0% -> 0%
where the time goes in v1:
time: 3370 us; the launch traced here: 3360 us
  waiting for transfers between devices  1480 us (44%)
  matrix products  668 us (20%)
  local copies, waits for them, and re-layouts  535 us (16%)
  blocking collectives  396 us (12%)
  other arithmetic  245 us (7%)
    unnamed x79, waiting for transfers between devices  527 us
    unnamed x722, local copies, waits for them, and re-layouts  483 us
    all_gather x6, waiting for transfers between devices, widen_rows(): lax.all_gather(as_sent(shards), 'tensor', axis=1, tiled=True)  188 us
    psum x12, blocking collectives, row_moments(): return lax.psum((values[0], values[1], values[2], values[3]), 'tensor')  182 us
    all_gather x6, waiting for transfers between devices, fold_back(): lax.all_gather(part, 'tensor', axis=1, tiled=True)  114 us
    convert_element_type x3, other arithmetic, attend_back(): grad_scores = (attn_probs * (grad_probs - row_dot)).astype(jnp.bfloat16)  90 us
    all_gather x6, blocking collectives, fold_back(): lax.all_gather(part, 'tensor', axis=1, tiled=True)  88.6 us
    all_gather x1, waiting for transfers between devices, gather_dense(): lax.all_gather(arrays[7], 'dp', axis=0, tiled=True)  85 us
  transfers between devices with their start and end apart: 62, of which 43 were waited for; matrix products, arithmetic and copies ran while one was open for 28% of the time, Pallas kernels for 0%

profile of v1, /device:TPU:0, one launch (start us, length us, event | category | flops | bytes accessed | tf_op | source)
XLA Modules:
  0.0 3357.8 jit_solution(2112940121210425742)
XLA Ops:
  13.2 41.9 %all-reduce.18.cloned.1.call-done = f32[2,4,18432]{2,0,1:T(2,128)} async-done(((f32[2,4,18432]{2,0,1:T(2,128)}), f32[2,4,18432]{2,0,1:T(2,128)}) %all-reduce.18.cloned.1.call-update) | async-done | bytes 589840
  116.1 56.0 %all-gather.55.cloned.1.call-done = bf16[1,3,1,384,1536]{4,3,1,2,0:T(8,128)(2,1)} async-done(((bf16[1,3,1,96,1536]{4,3,1,2,0:T(8,128)(2,1)}), bf16[1,3,1,384,1536]{4,3,1,2,0:T(8,128)(2,1)}) %all-gather.55.cloned.1.call-update) | async-done | bytes 3538960 | tf_op jit(solution)/shard_map/all_gather | solution.py:58
  175.3 66.7 %all-gather.53.cloned.1.call-done = bf16[1,3,1,384,1536]{4,3,1,2,0:T(8,128)(2,1)} async-done(((bf16[1,3,1,96,1536]{4,3,1,2,0:T(8,128)(2,1)}), bf16[1,3,1,384,1536]{4,3,1,2,0:T(8,128)(2,1)}) %all-gather.53.cloned.1.call-update) | async-done | bytes 3538960 | tf_op jit(solution)/shard_map/all_gather | solution.py:54
  242.0 44.6 %all-gather.29.cloned.1.call-done = bf16[1,1536,1024]{1,2,0:T(8,128)(2,1)} async-done(((bf16[1,384,1024]{1,2,0:T(8,128)(2,1)}), bf16[1,1536,1024]{1,2,0:T(8,128)(2,1)}) %all-gather.29.cloned.1.call-update) | async-done | bytes 3145744 | tf_op jit(solution)/shard_map/all_gather | solution.py:33
  383.1 44.7 %reduce-scatter.97.cloned.1.call-done = bf16[384,1024]{1,0:T(8,128)(2,1)} async-done(((bf16[1536,1024]{1,0:T(8,128)(2,1)}), bf16[384,1024]{1,0:T(8,128)(2,1)}) %reduce-scatter.97.cloned.1.call-update) | async-done | bytes 786448
  453.5 65.2 %all-gather.59.cloned.1.call-done = bf16[1,1536,1536]{2,1,0:T(8,128)(2,1)} async-done(((bf16[1,384,1536]{2,1,0:T(8,128)(2,1)}), bf16[1,1536,1536]{2,1,0:T(8,128)(2,1)}) %all-gather.59.cloned.1.call-update) | async-done | bytes 4718608 | tf_op jit(solution)/shard_map/all_gather | solution.py:56
  518.6 44.6 %all-gather.31.cloned.1.call-done = bf16[1,1536,1024]{1,2,0:T(8,128)(2,1)} async-done(((bf16[1,384,1024]{1,2,0:T(8,128)(2,1)}), bf16[1,1536,1024]{1,2,0:T(8,128)(2,1)}) %all-gather.31.cloned.1.call-update) | async-done | bytes 3145744 | tf_op jit(solution)/shard_map/all_gather | solution.py:33
  572.9 81.2 %all-gather.61.cloned.1.call-done = bf16[1,1536,1536]{2,1,0:T(8,128)(2,1)} async-done(((bf16[1,384,1536]{2,1,0:T(8,128)(2,1)}), bf16[1,1536,1536]{2,1,0:T(8,128)(2,1)}) %all-gather.61.cloned.1.call-update) | async-done | bytes 4718608 | tf_op jit(solution)/shard_map/all_gather | solution.py:57
  696.9 46.6 %all-gather.65.cloned.1.call-done = bf16[1,1536,1536]{2,1,0:T(8,128)(2,1)} async-done(((bf16[1,384,1536]{2,1,0:T(8,128)(2,1)}), bf16[1,1536,1536]{2,1,0:T(8,128)(2,1)}) %all-gather.65.cloned.1.call-update) | async-done | bytes 4718608 | tf_op jit(solution)/shard_map/all_gather | solution.py:60
  747.7 85.0 %all-gather.67.cloned.1.call-done = bf16[1,1536,1536]{2,1,0:T(8,128)(2,1)} async-done(((bf16[1,384,1536]{2,1,0:T(8,128)(2,1)}), bf16[1,1536,1536]{2,1,0:T(8,128)(2,1)}) %all-gather.67.cloned.1.call-update) | async-done | bytes 4718608 | tf_op jit(solution)/shard_map/all_gather | solution.py:61
  844.3 34.2 %reduce-scatter.99.cloned.1.call-done = bf16[384,1024]{1,0:T(8,128)(2,1)} async-done(((bf16[1536,1024]{1,0:T(8,128)(2,1)}), bf16[384,1024]{1,0:T(8,128)(2,1)}) %reduce-scatter.99.cloned.1.call-update) | async-done | bytes 786448
  1067.7 45.0 %reduce-scatter.105.cloned.1.call-done = bf16[384,1024]{1,0:T(8,128)(2,1)} async-done(((bf16[1536,1024]{1,0:T(8,128)(2,1)}), bf16[384,1024]{1,0:T(8,128)(2,1)}) %reduce-scatter.105.cloned.1.call-update) | async-done | bytes 786448
  1136.4 43.8 %all-gather.35.cloned.1.call-done = bf16[1,1536,1024]{1,2,0:T(8,128)(2,1)} async-done(((bf16[1,384,1024]{1,2,0:T(8,128)(2,1)}), bf16[1,1536,1024]{1,2,0:T(8,128)(2,1)}) %all-gather.35.cloned.1.call-update) | async-done | bytes 3145744 | tf_op jit(solution)/shard_map/all_gather | solution.py:33
  1462.7 45.1 %reduce-scatter.113.cloned.1.call-done = bf16[384,1024]{1,0:T(8,128)(2,1)} async-done(((bf16[1536,1024]{1,0:T(8,128)(2,1)}), bf16[384,1024]{1,0:T(8,128)(2,1)}) %reduce-scatter.113.cloned.1.call-update) | async-done | bytes 786448
  1728.4 32.6 reduce-scatter.115.cloned.1.call-done
  1989.7 41.4 %reduce-scatter.125.cloned.1.call-done = bf16[384,1024]{1,0:T(8,128)(2,1)} async-done(((bf16[1536,1024]{1,0:T(8,128)(2,1)}), bf16[384,1024]{1,0:T(8,128)(2,1)}) %reduce-scatter.125.cloned.1.call-update) | async-done | bytes 786448
  2161.2 39.7 %reduce-scatter.127.cloned.1.call-done = bf16[384,1024]{1,0:T(8,128)(2,1)} async-done(((bf16[1536,1024]{1,0:T(8,128)(2,1)}), bf16[384,1024]{1,0:T(8,128)(2,1)}) %reduce-scatter.127.cloned.1.call-update) | async-done | bytes 786448
  2423.7 41.4 %reduce-scatter.133.cloned.1.call-done = bf16[384,1024]{1,0:T(8,128)(2,1)} async-done(((bf16[1536,1024]{1,0:T(8,128)(2,1)}), bf16[384,1024]{1,0:T(8,128)(2,1)}) %reduce-scatter.133.cloned.1.call-update) | async-done | bytes 786448
  2593.9 41.3 %reduce-scatter.135.cloned.1.call-done = bf16[384,1024]{1,0:T(8,128)(2,1)} async-done(((bf16[1536,1024]{1,0:T(8,128)(2,1)}), bf16[384,1024]{1,0:T(8,128)(2,1)}) %reduce-scatter.135.cloned.1.call-update) | async-done | bytes 786448
  2964.7 43.5 %reduce-scatter.85.cloned.1.call-done = bf16[384,1536]{1,0:T(8,128)(2,1)} async-done(((bf16[1536,1536]{1,0:T(8,128)(2,1)}), bf16[384,1536]{1,0:T(8,128)(2,1)}) %reduce-scatter.85.cloned.1.call-update) | async-done | bytes 1179664 | tf_op jit(solution)/shard_map/reduce_scatter | solution.py:563
  3011.2 85.0 %reduce-scatter.87.cloned.1.call-done = bf16[384,1536]{1,0:T(8,128)(2,1)} async-done(((bf16[1536,1536]{1,0:T(8,128)(2,1)}), bf16[384,1536]{1,0:T(8,128)(2,1)}) %reduce-scatter.87.cloned.1.call-update) | async-done | bytes 1179664 | tf_op jit(solution)/shard_map/reduce_scatter | solution.py:566
  3159.8 44.3 %reduce-scatter.141.cloned.1.call-done = bf16[384,1024]{1,0:T(8,128)(2,1)} async-done(((bf16[1536,1024]{1,0:T(8,128)(2,1)}), bf16[384,1024]{1,0:T(8,128)(2,1)}) %reduce-scatter.141.cloned.1.call-update) | async-done | bytes 786448
  3231.1 49.9 %all_gather.140 = f32[16,2,1,2,6,384]{5,3,4,2,1,0:T(2,128)S(1)} all-gather(f32[1,2,1,2,6,384]{5,3,4,2,1,0:T(2,128)S(1)} %multiply_add_fusion), channel_id=1, replica_groups=mesh['pipe'=2,'dp'=4,'tensor'=4] {'dp','tensor'}, dimensions={0}, use_global_device_ids=true | all-gather | bytes 626688 | tf_op jit(solution)/shard_map/all_gather | solution.py:582
  3291.5 56.6 %reduce-scatter.89.cloned.1.call-done = bf16[3,96,1536]{2,1,0:T(8,128)(2,1)} async-done(((bf16[3,384,1536]{2,1,0:T(8,128)(2,1)}), bf16[3,96,1536]{2,1,0:T(8,128)(2,1)}) %reduce-scatter.89.cloned.1.call-update) | async-done | bytes 884752 | tf_op jit(solution)/shard_map/reduce_scatter | solution.py:569
  (1191 shorter events, 2118.0 us)
Async XLA Ops:
  58.2 183.8 %all-gather.53.cloned.1.call-start = ((), (), s32[]{:S(2)}) async-start(), calls=%async_computation.53 | async-start | bytes 4423680 | tf_op jit(solution)/shard_map/all_gather | solution.py:54
  58.8 227.8 %all-gather.29.cloned.1.call-start = ((), (), s32[]{:S(2)}) async-start(), calls=%async_computation.33 | async-start | bytes 3932160 | tf_op jit(solution)/shard_map/all_gather | solution.py:33
  103.0 243.8 %all-gather.63.cloned.1.call-start = ((), (), s32[]{:S(2)}) async-start(), calls=%async_computation.58 | async-start | bytes 1474560 | tf_op jit(solution)/shard_map/all_gather | solution.py:59
  103.6 250.6 %all-gather.57.cloned.1.call-start = ((), (), s32[]{:S(2)}) async-start(), calls=%async_computation.55 | async-start | bytes 1474560 | tf_op jit(solution)/shard_map/all_gather | solution.py:55
  104.3 276.8 %reduce-scatter.101.cloned.1.call-start = ((), (), s32[]{:S(2)}) async-start(), calls=%async_computation.63 | async-start | bytes 983040
  381.1 182.1 %all-gather.31.cloned.1.call-start = ((), (), s32[]{:S(2)}) async-start(), calls=%async_computation.34 | async-start | bytes 3932160 | tf_op jit(solution)/shard_map/all_gather | solution.py:33
  451.5 202.5 %all-gather.61.cloned.1.call-start = ((), (), s32[]{:S(2)}) async-start(), calls=%async_computation.57 | async-start | bytes 5898240 | tf_op jit(solution)/shard_map/all_gather | solution.py:57
  452.1 291.4 %all-gather.65.cloned.1.call-start = ((), (), s32[]{:S(2)}) async-start(), calls=%async_computation.59 | async-start | bytes 5898240 | tf_op jit(solution)/shard_map/all_gather | solution.py:60
  452.8 379.9 %all-gather.67.cloned.1.call-start = ((), (), s32[]{:S(2)}) async-start(), calls=%async_computation.60 | async-start | bytes 5898240 | tf_op jit(solution)/shard_map/all_gather | solution.py:61
  453.4 425.0 %reduce-scatter.99.cloned.1.call-start = ((), (), s32[]{:S(2)}) async-start(), calls=%async_computation.62 | async-start | bytes 3932160
  685.6 222.4 %reduce-scatter.103.cloned.1.call-start = ((), (), s32[]{:S(2)}) async-start(), calls=%async_computation.64 | async-start | bytes 983040
  1789.3 197.8 %reduce-scatter.129.cloned.1.call-start = ((), (), s32[]{:S(2)}) async-start(), calls=%async_computation.77 | async-start | bytes 983040
  2231.6 189.6 %reduce-scatter.137.cloned.1.call-start = ((), (), s32[]{:S(2)}) async-start(), calls=%async_computation.81 | async-start | bytes 983040
  2591.2 179.0 %all-gather.51.cloned.1.call-start = ((), (), s32[]{:S(2)}) async-start(), calls=%async_computation.44 | async-start | bytes 3932160 | tf_op jit(solution)/shard_map/all_gather | solution.py:182
  2665.9 291.0 %reduce-scatter.93.cloned.1.call-start = ((), (), s32[]{:S(2)}) async-start(), calls=%async_computation.51 | async-start | bytes 5898240 | tf_op jit(solution)/shard_map/reduce_scatter | solution.py:575
  2673.0 286.9 %reduce-scatter.95.cloned.1.call-start = ((), (), s32[]{:S(2)}) async-start(), calls=%async_computation.52 | async-start | bytes 5898240 | tf_op jit(solution)/shard_map/reduce_scatter | solution.py:578
  2682.0 280.8 %reduce-scatter.91.cloned.1.call-start = ((), (), s32[]{:S(2)}) async-start(), calls=%async_computation.50 | async-start | bytes 1474560 | tf_op jit(solution)/shard_map/reduce_scatter | solution.py:572
  2714.1 294.2 %reduce-scatter.85.cloned.1.call-start = ((), (), s32[]{:S(2)}) async-start(), calls=%async_computation.47 | async-start | bytes 5898240 | tf_op jit(solution)/shard_map/reduce_scatter | solution.py:563
  2732.2 364.0 %reduce-scatter.87.cloned.1.call-start = ((), (), s32[]{:S(2)}) async-start(), calls=%async_computation.48 | async-start | bytes 5898240 | tf_op jit(solution)/shard_map/reduce_scatter | solution.py:566
  2768.2 357.6 %reduce-scatter.143.cloned.1.call-start = ((), (), s32[]{:S(2)}) async-start(), calls=%async_computation.84 | async-start | bytes 983040
  2883.8 274.2 %reduce-scatter.83.cloned.1.call-start = ((), (), s32[]{:S(2)}) async-start(), calls=%async_computation.46 | async-start | bytes 1474560 | tf_op jit(solution)/shard_map/reduce_scatter | solution.py:560
  2890.1 314.0 %reduce-scatter.141.cloned.1.call-start = ((), (), s32[]{:S(2)}) async-start(), calls=%async_computation.83 | async-start | bytes 3932160
  2920.5 368.4 %reduce-scatter.81.cloned.1.call-start = ((), (), s32[]{:S(2)}) async-start(), calls=%async_computation.45 | async-start | bytes 4423680 | tf_op jit(solution)/shard_map/reduce_scatter | solution.py:557
  2947.2 400.8 %reduce-scatter.89.cloned.1.call-start = ((), (), s32[]{:S(2)}) async-start(), calls=%async_computation.49 | async-start | bytes 4423680 | tf_op jit(solution)/shard_map/reduce_scatter | solution.py:569
  (331 other events, 20293.3 us)
Sparse Core Ops, SparseCore 0:
  102.0 70.0 all-gather.54
  173.5 68.5 all-gather.52
  429.2 89.3 all-gather.58
  564.6 89.3 all-gather.60
  655.6 87.7 all-gather.64
  744.9 87.7 all-gather.66
  930.8 44.8 all-gather.32
  1068.8 43.8 reduce-scatter.104
  1221.5 46.2 reduce-scatter.106
  1463.9 43.8 reduce-scatter.112
  1531.5 48.3 all-gather.38
  1717.0 43.8 reduce-scatter.114
  1792.7 44.8 all-gather.42
  2065.4 47.6 all-gather.44
  2231.7 44.2 all-gather.46
  2500.5 46.7 all-gather.48
  2591.2 43.9 reduce-scatter.134
  2666.0 48.0 all-gather.50
  2716.2 85.2 reduce-scatter.92
  2803.7 85.7 reduce-scatter.94
  2924.3 83.8 reduce-scatter.84
  3010.4 85.7 reduce-scatter.86
  3206.2 71.8 reduce-scatter.80
  3280.4 67.5 reduce-scatter.88
  (30 shorter events, 1035.9 us)
